TPU v7x, 256 devices: a whole 4x4x8 slice. The times are simulated.
256 devices in a mesh: inl: 64 (over z, y, core), xl: 4 (over x).
Axes of the slice: x: 4, y: 4, z: 8, core: 2. Of those that a mesh axis runs over, the one named last changes fastest.
Arguments:
- traces: float32 [16384, 8, 1024], P(('inl', 'xl')), may hold values from -6 to 6
- owner: int32 [16384, 1], P(('inl', 'xl')), may hold values from 0 to 63; in each aligned block of 64 rows (0 to 63, 64 to 127, ...) at most 2 rows name the same one
- counts: int32 [16384], P(('inl', 'xl')), may hold values from 1 to 8, as said below
- inline_off: int32 [16384, 8], P(('inl', 'xl')), may hold values from 0 to 15
- xline_off: int32 [16384, 8], P(('inl', 'xl')), may hold values from 0 to 63
- phase_cls: int32 [16384, 8], P(('inl', 'xl')), may hold values from 0 to 15
Outputs:
- regular: bfloat16 [1024, 256, 2048], P('inl', 'xl')
Inputs may be any that keep to these rules, and one draw needn't show every extreme that they name: Among the blocks of one device, at most 2 name the same owner, a bound that some device reaches. `counts`: blocks whose index is 3 modulo 16 hold a single live trace, blocks whose index is 7 modulo 16 are full, all others hold 6 to 8 live traces.
All inputs are finite; a program needn't handle non-finite values.
Results may differ from a plain program's by a relative error of at most 0.0042.
Values sent between devices are 32-bit elements; how exact they have to be, the bound alone decides.
A program may use at most 64 MiB of HBM per device.

v0:
```python
import functools
import math

import jax
import jax.numpy as jnp
from jax import lax
from jax.experimental import pallas as pl
from jax.experimental.pallas import tpu as pltpu
from jax.sharding import PartitionSpec as P

XLINES = 256
TAPS = 8
PHASES = 16
BLOCK_TR = 8
SLOTS = 2
IL_DEV = 16
CHUNKS = 4
CAP = 3
LANES = 128
ROWS = SLOTS * BLOCK_TR
MESH = pl.DeviceIdType.MESH


def sinc_table():
    phase_idx = jnp.arange(PHASES, dtype=jnp.int32).astype(jnp.float32)[:, None]
    tap_idx = jnp.arange(TAPS, dtype=jnp.int32).astype(jnp.float32)[None, :]
    offset = tap_idx - 3.0 - phase_idx / PHASES
    return jnp.sinc(offset) * (0.5 + 0.5 * jnp.cos(math.pi * offset / 4.0))


def wait_for(ref, sem):
    pltpu.make_async_copy(ref, ref, sem).wait()


def build_resample(table_ref):
    length, width = table_ref.shape
    step = 16

    def body(part, carry):
        base = pl.multiple_of(part * step, step)
        rows_idx = lax.broadcasted_iota(jnp.int32, (step, width), 0) + base
        cols_idx = lax.broadcasted_iota(jnp.int32, (step, width), 1)
        lagged = (cols_idx >> 1) - rows_idx
        sign_val = (1 - 2 * (lagged & 1)).astype(jnp.float32)
        odd_val = sign_val / (math.pi * (lagged.astype(jnp.float32) + 0.5))
        even_val = (lagged == 0).astype(jnp.float32)
        table_ref[pl.ds(base, step), :] = jnp.where((cols_idx & 1) == 1, odd_val, even_val).astype(
            jnp.bfloat16
        )
        return carry

    lax.fori_loop(0, length // step, body, 0)


def padded_kernel(
    n_inl,
    n_xl,
    index_ref,
    traces_hbm,
    nav_ref,
    taps_ref,
    out_hbm,
    traces,
    send,
    recv,
    nav_send,
    nav_recv,
    inner,
    outer_f32,
    outer,
    resample,
    total,
    stack,
    out_rows,
    halo_send,
    halo_recv,
    fold_in,
    fold_send,
    fold_recv,
    load_sem,
    send_sems,
    recv_sems,
    nav_send_sem,
    nav_recv_sem,
    halo_send_sems,
    halo_recv_sems,
    fold_send_sems,
    fold_recv_sems,
    out_sem,
):
    me = lax.axis_index("inl")
    band = lax.axis_index("xl")
    right, left = lax.rem(band + 1, n_xl), lax.rem(band + n_xl - 1, n_xl)
    chunk = traces.shape[2] // CHUNKS
    depth = n_inl * ROWS
    width = inner.shape[0] // IL_DEV
    padded = width + 2 * TAPS
    side = IL_DEV * TAPS

    load = pltpu.make_async_copy(traces_hbm, traces, load_sem)
    load.start()

    barrier = pltpu.get_barrier_semaphore()

    def greet(off, carry):
        dest = lax.rem(me + off, n_inl)
        pl.semaphore_signal(barrier, inc=1, device_id={"inl": dest}, device_id_type=MESH)
        return carry

    lax.fori_loop(1, n_inl, greet, 0)
    for neighbour in (left, right):
        pl.semaphore_signal(barrier, inc=1, device_id={"xl": neighbour}, device_id_type=MESH)

    def gather_nav(off, carry):
        dest = lax.rem(me + off, n_inl)
        for slot in range(SLOTS):
            block = index_ref[dest, slot]
            nav_send[dest, slot * BLOCK_TR : (slot + 1) * BLOCK_TR, :] = nav_ref[block]
        return carry

    lax.fori_loop(0, n_inl, gather_nav, 0)
    nav_recv[me] = nav_send[me]
    load.wait()

    def gather(c):
        def body(off, carry):
            dest = lax.rem(me + off, n_inl)
            for slot in range(SLOTS):
                block = index_ref[dest, SLOTS + slot]
                send[c, dest, slot * BLOCK_TR : (slot + 1) * BLOCK_TR, :] = traces[
                    block, :, c * chunk : (c + 1) * chunk
                ]
            return carry

        lax.fori_loop(0, n_inl, body, 0)
        recv[c, me] = send[c, me]

    gather(0)
    pl.semaphore_wait(barrier, n_inl - 1 + 2)

    def push_nav(off, carry):
        dest = lax.rem(me + off, n_inl)
        pltpu.make_async_remote_copy(
            src_ref=nav_send.at[dest],
            dst_ref=nav_recv.at[me],
            send_sem=nav_send_sem,
            recv_sem=nav_recv_sem,
            device_id={"inl": dest},
            device_id_type=MESH,
        ).start()
        return carry

    lax.fori_loop(1, n_inl, push_nav, 0)

    def push(c):
        def body(off, carry):
            dest = lax.rem(me + off, n_inl)
            pltpu.make_async_remote_copy(
                src_ref=send.at[c, dest],
                dst_ref=recv.at[c, me],
                send_sem=send_sems.at[c],
                recv_sem=recv_sems.at[c],
                device_id={"inl": dest},
                device_id_type=MESH,
            ).start()
            return carry

        lax.fori_loop(1, n_inl, body, 0)

    for c in range(CHUNKS):
        if c + 1 < CHUNKS:
            gather(c + 1)
        push(c)

    build_resample(resample)

    wait_for(nav_recv.at[pl.ds(0, n_inl - 1)], nav_recv_sem)
    nav = nav_recv[...].reshape(depth, LANES).T
    inl_ids, xl_ids, cls_ids, live = nav[0:1], nav[1:2], nav[2:3], nav[3:4]
    weights = jnp.zeros((TAPS, depth), jnp.float32)
    for phase in range(PHASES):
        weights = jnp.where(cls_ids == float(phase), taps_ref[:, phase : phase + 1], weights)
    weights = weights * live
    tap_of = lax.broadcasted_iota(jnp.int32, (padded, depth), 0).astype(jnp.float32) - (xl_ids + 5.0)
    spread = jnp.zeros((padded, depth), jnp.float32)
    for tap in range(TAPS):
        spread = jnp.where(tap_of == float(tap), weights[tap : tap + 1], spread)

    def line(i, carry):
        rows = jnp.where(inl_ids == i.astype(jnp.float32), spread, 0.0)
        sums = jnp.broadcast_to(jnp.sum(rows, axis=1, keepdims=True), (padded, LANES))
        base = pl.multiple_of(i * width, width)
        inner[pl.ds(base, width), :] = rows[TAPS : TAPS + width].astype(jnp.bfloat16)
        fold_in[pl.ds(base, width), :] = sums[TAPS : TAPS + width]
        edge = pl.multiple_of(i * TAPS, TAPS)
        outer_f32[0, pl.ds(edge, TAPS), :] = rows[:TAPS]
        outer_f32[1, pl.ds(edge, TAPS), :] = rows[TAPS + width :]
        fold_send[0, pl.ds(edge, TAPS), :] = sums[:TAPS]
        fold_send[1, pl.ds(edge, TAPS), :] = sums[TAPS + width :]
        return carry

    lax.fori_loop(0, IL_DEV, line, 0)
    outer[...] = outer_f32[...].astype(jnp.bfloat16).reshape(2 * side, depth)

    folds = []
    for way, neighbour in ((0, left), (1, right)):
        copy = pltpu.make_async_remote_copy(
            src_ref=fold_send.at[way],
            dst_ref=fold_recv.at[way],
            send_sem=fold_send_sems.at[way],
            recv_sem=fold_recv_sems.at[way],
            device_id={"xl": neighbour},
            device_id_type=MESH,
        )
        copy.start()
        folds.append(copy)

    from_right = jnp.where(band < n_xl - 1, 1.0, 0.0)
    from_left = jnp.where(band > 0, 1.0, 0.0)

    for copy in folds:
        copy.wait()

    def join(i, carry):
        edge = pl.multiple_of(i * TAPS, TAPS)
        first = pl.multiple_of(i * width, TAPS)
        last = pl.multiple_of(i * width + width - TAPS, TAPS)
        fold_in[pl.ds(last, TAPS), :] += fold_recv[0, pl.ds(edge, TAPS), :] * from_right
        fold_in[pl.ds(first, TAPS), :] += fold_recv[1, pl.ds(edge, TAPS), :] * from_left
        return carry

    lax.fori_loop(0, IL_DEV, join, 0)
    fold_in[...] = 1.0 / jnp.maximum(fold_in[...], 0.25)

    halos = []
    for c in range(CHUNKS):
        wait_for(recv.at[c, pl.ds(0, n_inl - 1)], recv_sems.at[c])
        block = recv[c].reshape(depth, chunk).astype(jnp.bfloat16)
        halo_send[c] = jnp.dot(outer[...], block, preferred_element_type=jnp.float32).reshape(
            2, side, chunk
        )
        stack[...] = jnp.dot(inner[...], block, preferred_element_type=jnp.float32)
        sent = []
        for way, neighbour in ((0, left), (1, right)):
            copy = pltpu.make_async_remote_copy(
                src_ref=halo_send.at[c, way],
                dst_ref=halo_recv.at[c, way],
                send_sem=halo_send_sems.at[c, way],
                recv_sem=halo_recv_sems.at[c, way],
                device_id={"xl": neighbour},
                device_id_type=MESH,
            )
            copy.start()
            sent.append(copy)
        for copy in sent:
            copy.wait()

        def add_halo(i, carry, c=c):
            edge = pl.multiple_of(i * TAPS, TAPS)
            first = pl.multiple_of(i * width, TAPS)
            last = pl.multiple_of(i * width + width - TAPS, TAPS)
            stack[pl.ds(last, TAPS), :] += halo_recv[c, 0, pl.ds(edge, TAPS), :] * from_right
            stack[pl.ds(first, TAPS), :] += halo_recv[c, 1, pl.ds(edge, TAPS), :] * from_left
            return carry

        lax.fori_loop(0, IL_DEV, add_halo, 0)

        tile = out_rows.shape[0] // TAPS

        def finish(m, carry, c=c):
            base = pl.multiple_of(m * tile, tile)
            scale = fold_in[pl.ds(base, tile), 0:1]
            binned = (stack[pl.ds(base, tile), :] * scale).astype(jnp.bfloat16)
            part = jnp.dot(
                binned, resample[c * chunk : (c + 1) * chunk, :], preferred_element_type=jnp.float32
            )
            if c > 0:
                part = part + total[pl.ds(base, tile), :]
            if c < CHUNKS - 1:
                total[pl.ds(base, tile), :] = part
            else:
                out_rows[pl.ds(base, tile), :] = part.astype(jnp.bfloat16)
                pltpu.make_async_copy(
                    out_rows.at[pl.ds(base, tile)], out_hbm.at[pl.ds(base, tile)], out_sem
                ).start()
            return carry

        lax.fori_loop(0, TAPS, finish, 0)

    wait_for(nav_send.at[pl.ds(0, n_inl - 1)], nav_send_sem)
    for c in range(CHUNKS):
        wait_for(send.at[c, pl.ds(0, n_inl - 1)], send_sems.at[c])
    wait_for(out_rows, out_sem)


def padded_plan(traces, owner, counts, inline_off, xline_off, phase_cls):
    n_inl, n_xl = lax.axis_size("inl"), lax.axis_size("xl")
    local_blocks, _, samples = traces.shape
    width = XLINES // n_xl
    chunk = samples // CHUNKS
    depth = n_inl * ROWS
    side = IL_DEV * TAPS
    block_idx = jnp.arange(local_blocks, dtype=jnp.int32)
    named = owner[:, 0][None, :] == jnp.arange(n_inl, dtype=jnp.int32)[:, None]
    low = jnp.min(jnp.where(named, block_idx[None, :], local_blocks), axis=1)
    high = jnp.max(jnp.where(named, block_idx[None, :], -1), axis=1)
    high = jnp.where(high > low, high, local_blocks)
    nav_index = jnp.stack([low, high], axis=1)
    index = jnp.concatenate([nav_index, jnp.minimum(nav_index, local_blocks - 1)], axis=1)
    live = (jnp.arange(BLOCK_TR, dtype=jnp.int32)[None, :] < counts[:, None]).astype(jnp.float32)
    parts = [inline_off.astype(jnp.float32), xline_off.astype(jnp.float32)]
    parts = parts + [phase_cls.astype(jnp.float32), live]
    nav = jnp.stack(parts, axis=2)
    nav = jnp.pad(nav, ((0, 1), (0, 0), (0, LANES - len(parts))))
    taps = sinc_table().T
    scratch = [
        pltpu.VMEM((local_blocks, BLOCK_TR, samples), jnp.float32),
        pltpu.VMEM((CHUNKS, n_inl, ROWS, chunk), jnp.float32),
        pltpu.VMEM((CHUNKS, n_inl, ROWS, chunk), jnp.float32),
        pltpu.VMEM((n_inl, ROWS, LANES), jnp.float32),
        pltpu.VMEM((n_inl, ROWS, LANES), jnp.float32),
        pltpu.VMEM((IL_DEV * width, depth), jnp.bfloat16),
        pltpu.VMEM((2, side, depth), jnp.float32),
        pltpu.VMEM((2 * side, depth), jnp.bfloat16),
        pltpu.VMEM((samples, 2 * samples), jnp.bfloat16),
        pltpu.VMEM((IL_DEV * width, 2 * samples), jnp.float32),
        pltpu.VMEM((IL_DEV * width, chunk), jnp.float32),
        pltpu.VMEM((IL_DEV * width, 2 * samples), jnp.bfloat16),
        pltpu.VMEM((CHUNKS, 2, side, chunk), jnp.float32),
        pltpu.VMEM((CHUNKS, 2, side, chunk), jnp.float32),
        pltpu.VMEM((IL_DEV * width, LANES), jnp.float32),
        pltpu.VMEM((2, side, LANES), jnp.float32),
        pltpu.VMEM((2, side, LANES), jnp.float32),
        pltpu.SemaphoreType.DMA,
        pltpu.SemaphoreType.DMA((CHUNKS,)),
        pltpu.SemaphoreType.DMA((CHUNKS,)),
        pltpu.SemaphoreType.DMA,
        pltpu.SemaphoreType.DMA,
        pltpu.SemaphoreType.DMA((CHUNKS, 2)),
        pltpu.SemaphoreType.DMA((CHUNKS, 2)),
        pltpu.SemaphoreType.DMA((2,)),
        pltpu.SemaphoreType.DMA((2,)),
        pltpu.SemaphoreType.DMA,
    ]
    out = pl.pallas_call(
        functools.partial(padded_kernel, n_inl, n_xl),
        out_shape=jax.ShapeDtypeStruct((IL_DEV * width, 2 * samples), jnp.bfloat16),
        in_specs=[
            pl.BlockSpec(memory_space=pltpu.SMEM),
            pl.BlockSpec(memory_space=pl.ANY),
            pl.BlockSpec(memory_space=pltpu.VMEM),
            pl.BlockSpec(memory_space=pltpu.VMEM),
        ],
        out_specs=pl.BlockSpec(memory_space=pl.ANY),
        scratch_shapes=scratch,
        compiler_params=pltpu.CompilerParams(
            collective_id=1, has_side_effects=True, vmem_limit_bytes=44 << 20
        ),
    )(index, traces, nav, taps)
    return out.reshape(IL_DEV, width, 2 * samples)


EDGES = (0, 3, 5, 7, 8)
PARTS = len(EDGES) - 1


def span_of(c, length):
    return EDGES[c] * length // EDGES[-1], EDGES[c + 1] * length // EDGES[-1]


def widest(length):
    return max(hi - lo for lo, hi in [span_of(c, length) for c in range(PARTS)])


def plane_of(n_inl):
    return 8 if n_inl % 8 == 0 and n_inl > 8 else 2


def plan_kernel(n_inl, owner_ref, counts_ref, inl_ref, xl_ref, cls_ref, table_ref, nav_ref, taps_ref):
    blocks = owner_ref.shape[1]
    plane = plane_of(n_inl)
    named = owner_ref[...] == lax.broadcasted_iota(jnp.int32, (n_inl, blocks), 0)
    block_idx = lax.broadcasted_iota(jnp.int32, (n_inl, blocks), 1).astype(jnp.float32)
    low = jnp.min(jnp.where(named, block_idx, float(blocks)), axis=1, keepdims=True)
    high = jnp.max(jnp.where(named, block_idx, -1.0), axis=1, keepdims=True)
    two = jnp.broadcast_to(jnp.where(high > low, 1.0, 0.0), (n_inl, LANES))
    row_id = lax.broadcasted_iota(jnp.int32, (n_inl, n_inl), 0)
    col_id = lax.broadcasted_iota(jnp.int32, (n_inl, n_inl), 1)
    ahead = jnp.where((col_id < row_id) & (col_id // plane == row_id // plane), 1.0, 0.0)
    rank = jnp.dot(ahead, two, preferred_element_type=jnp.float32)
    own = lax.broadcasted_iota(jnp.int32, (n_inl, LANES), 0)
    lane = lax.broadcasted_iota(jnp.int32, (n_inl, LANES), 1)
    slot = (own // plane * CAP).astype(jnp.float32) + rank
    chosen = (two > 0.5) & (rank < CAP - 0.5) & (slot == lane.astype(jnp.float32))
    taken = jnp.sum(jnp.where(chosen, 1.0, 0.0), axis=0, keepdims=True)
    second = jnp.sum(jnp.where(chosen, high, 0.0), axis=0, keepdims=True)
    second = jnp.where(taken > 0.5, second, float(blocks))
    target = jnp.where(chosen, (own % plane + 1).astype(jnp.float32), 0.0)
    target = jnp.sum(target, axis=0, keepdims=True)
    over = jnp.where((two > 0.5) & (rank > CAP - 0.5), 1.0, 0.0)
    over = jnp.max(over, axis=0, keepdims=True)
    table_ref[:n_inl, :] = jnp.broadcast_to(low, (n_inl, LANES)).astype(jnp.int32)
    table_ref[n_inl : n_inl + 1, :] = second.astype(jnp.int32)
    table_ref[n_inl + 1 : n_inl + 2, :] = target.astype(jnp.int32)
    table_ref[n_inl + 2 : n_inl + 3, :] = over.astype(jnp.int32)
    table_ref[n_inl + 3 :, :] = jnp.zeros((5, LANES), jnp.int32)
    tap = lax.broadcasted_iota(jnp.int32, (TAPS, LANES), 0).astype(jnp.float32)
    offset = tap - 3.0 - lax.broadcasted_iota(jnp.int32, (TAPS, LANES), 1).astype(jnp.float32) / PHASES
    at_zero = offset == 0.0
    angle = math.pi * jnp.where(at_zero, 1.0, offset)
    sinc = jnp.where(at_zero, 1.0, jnp.sin(angle) / angle)
    taps_ref[...] = sinc * (0.5 + 0.5 * jnp.cos(math.pi * offset / 4.0))
    trace_idx = lax.broadcasted_iota(jnp.int32, (BLOCK_TR, blocks), 0)
    fields = [inl_ref[...], xl_ref[...], cls_ref[...], (trace_idx < counts_ref[...]).astype(jnp.int32)]
    fields = [field.astype(jnp.float32) for field in fields]
    field_id = lax.broadcasted_iota(jnp.int32, (BLOCK_TR, LANES), 1)
    for block in range(blocks):
        tile = jnp.zeros((BLOCK_TR, LANES), jnp.float32)
        for place, field in enumerate(fields):
            tile = jnp.where(field_id == place, field[:, block : block + 1], tile)
        nav_ref[block] = tile
    nav_ref[blocks] = jnp.zeros((BLOCK_TR, LANES), jnp.float32)


def fast_kernel(
    n_inl,
    n_xl,
    table_ref,
    traces_hbm,
    nav_ref,
    taps_ref,
    total,
    tail_ref,
    binned_ref,
    flag_ref,
    traces,
    p_send,
    p_recv,
    z_send,
    z_recv,
    y_send,
    y_recv,
    p_nav_send,
    p_nav_recv,
    z_nav_send,
    z_nav_recv,
    y_nav_send,
    y_nav_recv,
    samples_in,
    inner,
    outer_f32,
    outer,
    resample,
    stack,
    halo_send,
    halo_recv,
    fold_in,
    fold_send,
    fold_recv,
    flag_send,
    flag_recv,
    load_sem,
    p_sems,
    z_sems,
    y_sems,
    nav_sems,
    halo_sems,
    fold_sems,
    flag_sems,
):
    me = lax.axis_index("inl")
    band = lax.axis_index("xl")
    plane = plane_of(n_inl)
    layers = n_inl // plane
    layer, place = me // plane, lax.rem(me, plane)
    right, left = lax.rem(band + 1, n_xl), lax.rem(band + n_xl - 1, n_xl)
    length = traces.shape[2]
    blocks = traces.shape[0]
    half = n_inl * BLOCK_TR
    depth = 2 * half
    width = inner.shape[0] // IL_DEV
    padded = width + 2 * TAPS
    side = IL_DEV * TAPS

    load = pltpu.make_async_copy(traces_hbm, traces, load_sem)
    load.start()

    barrier = pltpu.get_barrier_semaphore()

    def greet(off, carry):
        dest = lax.rem(me + 1 + lax.rem(off + n_inl * 7 // 16, n_inl - 1), n_inl)
        pl.semaphore_signal(barrier, inc=1, device_id={"inl": dest}, device_id_type=MESH)
        return carry

    lax.fori_loop(0, n_inl - 1, greet, 0)
    for step in range(1, n_xl):
        other = lax.rem(band + step, n_xl)
        pl.semaphore_signal(barrier, inc=1, device_id={"xl": other}, device_id_type=MESH)

    field_id = lax.broadcasted_iota(jnp.int32, (BLOCK_TR, LANES), 1)
    over = table_ref[n_inl + 2, 0].astype(jnp.float32)
    load.wait()

    def gather_second(layer_to, carry):
        for r in range(CAP):
            spot = layer_to * CAP + r
            block = table_ref[n_inl, spot]
            target = table_ref[n_inl + 1, spot].astype(jnp.float32)
            z_nav_send[layer_to, r] = jnp.where(field_id == 4, target, nav_ref[block])
            z_send[layer_to, r * BLOCK_TR : (r + 1) * BLOCK_TR, :] = traces[
                jnp.minimum(block, blocks - 1)
            ]
        return carry

    lax.fori_loop(0, layers, gather_second, 0)

    def gather_first(off, carry):
        dest = lax.rem(me + off, n_inl)
        block = table_ref[dest, 0]
        p_nav_send[dest] = jnp.where(field_id == 5, over, nav_ref[block])
        p_send[dest] = traces[jnp.minimum(block, blocks - 1)]
        return carry

    lax.fori_loop(0, n_inl, gather_first, 0)
    p_nav_recv[me] = p_nav_send[me]
    p_recv[me] = p_send[me]
    z_nav_recv[layer] = z_nav_send[layer]
    z_recv[layer] = z_send[layer]

    pl.semaphore_wait(barrier, n_inl - 1 + n_xl - 1)

    def span(c):
        lo, hi = span_of(c, length)
        return pl.ds(lo, hi - lo)

    def push(source, target, sems, to):
        pltpu.make_async_remote_copy(
            src_ref=source,
            dst_ref=target,
            send_sem=sems[0],
            recv_sem=sems[1],
            device_id=to,
            device_id_type=MESH,
        ).start()

    def push_first(c):
        def body(off, carry):
            dest = lax.rem(me + off, n_inl)
            push(
                p_send.at[dest, :, span(c)],
                p_recv.at[me, :, span(c)],
                (p_sems.at[0, c], p_sems.at[1, c]),
                {"inl": dest},
            )
            return carry

        lax.fori_loop(1, n_inl, body, 0)

    def push_second(c):
        def body(off, carry):
            to = lax.rem(layer + off, layers)
            push(
                z_send.at[to, :, span(c)],
                z_recv.at[layer, :, span(c)],
                (z_sems.at[0, c], z_sems.at[1, c]),
                {"inl": to * plane + place},
            )
            return carry

        lax.fori_loop(1, layers, body, 0)

    def spread_second(c):
        lo, hi = span_of(c, length)
        wait_for(z_recv.at[pl.ds(0, layers - 1), :, span(c)], z_sems.at[1, c])

        def body(to, carry):
            wanted = (to + 1).astype(jnp.float32)
            for origin in range(layers):
                held = jnp.zeros((BLOCK_TR, hi - lo), jnp.float32)
                for r in range(CAP):
                    named = z_nav_recv[origin, r, :, 4:5] == wanted
                    value = z_recv[origin, r * BLOCK_TR : (r + 1) * BLOCK_TR, lo:hi]
                    held = jnp.where(named, value, held)
                y_send[to, origin * BLOCK_TR : (origin + 1) * BLOCK_TR, lo:hi] = held
            return carry

        lax.fori_loop(0, plane, body, 0)
        y_recv[place, :, lo:hi] = y_send[place, :, lo:hi]

        def send(off, carry):
            to = lax.rem(place + off, plane)
            push(
                y_send.at[to, :, span(c)],
                y_recv.at[place, :, span(c)],
                (y_sems.at[0, c], y_sems.at[1, c]),
                {"inl": layer * plane + to},
            )
            return carry

        lax.fori_loop(1, plane, send, 0)

    def push_z_nav(off, carry):
        to = lax.rem(layer + off, layers)
        push(
            z_nav_send.at[to],
            z_nav_recv.at[layer],
            (nav_sems.at[0, 1], nav_sems.at[1, 1]),
            {"inl": to * plane + place},
        )
        return carry

    def push_p_nav(off, carry):
        dest = lax.rem(me + off, n_inl)
        push(
            p_nav_send.at[dest],
            p_nav_recv.at[me],
            (nav_sems.at[0, 0], nav_sems.at[1, 0]),
            {"inl": dest},
        )
        return carry

    push_second(0)
    lax.fori_loop(1, layers, push_z_nav, 0)
    push_second(1)
    push_first(0)
    lax.fori_loop(1, n_inl, push_p_nav, 0)
    push_second(2)
    push_first(1)

    wait_for(z_nav_recv.at[pl.ds(0, layers - 1)], nav_sems.at[1, 1])

    def spread_nav(to, carry):
        wanted = (to + 1).astype(jnp.float32)
        for origin in range(layers):
            held = jnp.zeros((BLOCK_TR, LANES), jnp.float32)
            for r in range(CAP):
                tile = z_nav_recv[origin, r]
                held = jnp.where(tile[:, 4:5] == wanted, tile, held)
            y_nav_send[to, origin] = held
        return carry

    lax.fori_loop(0, plane, spread_nav, 0)
    y_nav_recv[place] = y_nav_send[place]

    def push_y_nav(off, carry):
        to = lax.rem(place + off, plane)
        push(
            y_nav_send.at[to],
            y_nav_recv.at[place],
            (nav_sems.at[0, 2], nav_sems.at[1, 2]),
            {"inl": layer * plane + to},
        )
        return carry

    lax.fori_loop(1, plane, push_y_nav, 0)
    spread_second(0)
    build_resample(resample)
    tail_ref[...] = resample[span_of(PARTS - 1, length)[0] :, :]
    spread_second(1)
    push_second(3)
    push_first(2)

    wait_for(p_nav_recv.at[pl.ds(0, n_inl - 1)], nav_sems.at[1, 0])
    wait_for(y_nav_recv.at[pl.ds(0, plane - 1)], nav_sems.at[1, 2])
    first_nav = p_nav_recv[...].reshape(half, LANES).T
    second_nav = y_nav_recv[...].reshape(half, LANES).T
    nav = jnp.concatenate([first_nav[:8], second_nav[:8]], axis=1)
    inl_ids, xl_ids, cls_ids, live = nav[0:1], nav[1:2], nav[2:3], nav[3:4]

    seen = jnp.max(first_nav[5:6], axis=1, keepdims=True)
    flag_send[...] = jnp.broadcast_to(seen, (BLOCK_TR, LANES))
    flag_recv[0] = flag_send[...]
    for step in range(1, n_xl):
        other = lax.rem(band + step, n_xl)
        push(flag_send, flag_recv.at[step], (flag_sems.at[0, step], flag_sems.at[1, step]), {"xl": other})

    weights = jnp.zeros((TAPS, depth), jnp.float32)
    for phase in range(PHASES):
        weights = jnp.where(cls_ids == float(phase), taps_ref[:, phase : phase + 1], weights)
    weights = weights * live
    tap_of = lax.broadcasted_iota(jnp.int32, (padded, depth), 0).astype(jnp.float32) - (xl_ids + 5.0)
    spread = jnp.zeros((padded, depth), jnp.float32)
    for tap in range(TAPS):
        spread = jnp.where(tap_of == float(tap), weights[tap : tap + 1], spread)

    def line(i, carry):
        rows = jnp.where(inl_ids == i.astype(jnp.float32), spread, 0.0)
        sums = jnp.broadcast_to(jnp.sum(rows, axis=1, keepdims=True), (padded, LANES))
        base = pl.multiple_of(i * width, width)
        inner[pl.ds(base, width), :] = rows[TAPS : TAPS + width].astype(jnp.bfloat16)
        fold_in[pl.ds(base, width), :] = sums[TAPS : TAPS + width]
        edge = pl.multiple_of(i * TAPS, TAPS)
        outer_f32[0, pl.ds(edge, TAPS), :] = rows[:TAPS]
        outer_f32[1, pl.ds(edge, TAPS), :] = rows[TAPS + width :]
        fold_send[0, pl.ds(edge, TAPS), :] = sums[:TAPS]
        fold_send[1, pl.ds(edge, TAPS), :] = sums[TAPS + width :]
        return carry

    lax.fori_loop(0, IL_DEV, line, 0)
    outer[...] = outer_f32[...].astype(jnp.bfloat16).reshape(2 * side, depth)

    for way, neighbour in ((0, left), (1, right)):
        push(
            fold_send.at[way],
            fold_recv.at[way],
            (fold_sems.at[0, way], fold_sems.at[1, way]),
            {"xl": neighbour},
        )

    from_right = jnp.where(band < n_xl - 1, 1.0, 0.0)
    from_left = jnp.where(band > 0, 1.0, 0.0)

    spread_second(2)
    push_first(3)

    for way in range(2):
        wait_for(fold_recv.at[way], fold_sems.at[1, way])

    def join(i, carry):
        edge = pl.multiple_of(i * TAPS, TAPS)
        first = pl.multiple_of(i * width, TAPS)
        last = pl.multiple_of(i * width + width - TAPS, TAPS)
        fold_in[pl.ds(last, TAPS), :] += fold_recv[0, pl.ds(edge, TAPS), :] * from_right
        fold_in[pl.ds(first, TAPS), :] += fold_recv[1, pl.ds(edge, TAPS), :] * from_left
        return carry

    lax.fori_loop(0, IL_DEV, join, 0)
    fold_in[...] = 1.0 / jnp.maximum(fold_in[...], 0.25)

    for step in range(1, n_xl):
        wait_for(flag_recv.at[step], flag_sems.at[1, step])
    flag_ref[...] = jnp.max(flag_recv[...], axis=0)

    def stage(c):
        lo, hi = span_of(c, length)
        size = hi - lo
        wait_for(y_recv.at[pl.ds(0, plane - 1), :, span(c)], y_sems.at[1, c])
        samples_in[half:, :size] = y_recv[:, :, lo:hi].reshape(half, size).astype(jnp.bfloat16)
        wait_for(p_recv.at[pl.ds(0, n_inl - 1), :, span(c)], p_sems.at[1, c])
        samples_in[:half, :size] = p_recv[:, :, lo:hi].reshape(half, size).astype(jnp.bfloat16)
        halo_send[:, :, lo:hi] = jnp.dot(
            outer[...], samples_in[:, :size], preferred_element_type=jnp.float32
        ).reshape(2, side, size)
        for way, neighbour in ((0, left), (1, right)):
            push(
                halo_send.at[way, :, span(c)],
                halo_recv.at[way, :, span(c)],
                (halo_sems.at[0, c, way], halo_sems.at[1, c, way]),
                {"xl": neighbour},
            )
        stack[:, lo:hi] = jnp.dot(
            inner[...], samples_in[:, :size], preferred_element_type=jnp.float32
        )

    def finish(c):
        lo, hi = span_of(c, length)
        for way in range(2):
            wait_for(halo_recv.at[way, :, span(c)], halo_sems.at[1, c, way])
        tile = 2 * width

        def body(m, carry):
            base = pl.multiple_of(m * tile, tile)
            for i in range(2):
                edge = pl.multiple_of(m * 2 * TAPS + i * TAPS, TAPS)
                first = pl.multiple_of(base + i * width, TAPS)
                last = pl.multiple_of(base + i * width + width - TAPS, TAPS)
                stack[pl.ds(last, TAPS), lo:hi] += halo_recv[0, pl.ds(edge, TAPS), lo:hi] * from_right
                stack[pl.ds(first, TAPS), lo:hi] += halo_recv[1, pl.ds(edge, TAPS), lo:hi] * from_left
            scale = fold_in[pl.ds(base, tile), 0:1]
            binned = (stack[pl.ds(base, tile), lo:hi] * scale).astype(jnp.bfloat16)
            if c == PARTS - 1:
                binned_ref[pl.ds(base, tile), :] = binned
                return carry
            part = jnp.dot(binned, resample[lo:hi, :], preferred_element_type=jnp.float32)
            if c > 0:
                part = part + total[pl.ds(base, tile), :]
            total[pl.ds(base, tile), :] = part
            return carry

        lax.fori_loop(0, IL_DEV // 2, body, 0)

    stage(0)
    finish(0)
    stage(1)
    spread_second(3)
    finish(1)
    stage(2)
    stage(3)
    finish(2)
    finish(3)

    wait_for(p_nav_send.at[pl.ds(0, n_inl - 1)], nav_sems.at[0, 0])
    wait_for(z_nav_send.at[pl.ds(0, layers - 1)], nav_sems.at[0, 1])
    wait_for(y_nav_send.at[pl.ds(0, plane - 1)], nav_sems.at[0, 2])
    for c in range(PARTS):
        wait_for(p_send.at[pl.ds(0, n_inl - 1), :, span(c)], p_sems.at[0, c])
        wait_for(z_send.at[pl.ds(0, layers - 1), :, span(c)], z_sems.at[0, c])
        wait_for(y_send.at[pl.ds(0, plane - 1), :, span(c)], y_sems.at[0, c])
        for way in range(2):
            wait_for(halo_send.at[way, :, span(c)], halo_sems.at[0, c, way])
    for way in range(2):
        wait_for(fold_send.at[way], fold_sems.at[0, way])
    for step in range(1, n_xl):
        wait_for(flag_send, flag_sems.at[0, step])


def finish_kernel(total_ref, binned_ref, tail_ref, out_hbm, rows, sem):
    tile = rows.shape[0] // 8

    def body(m, carry):
        base = pl.multiple_of(m * tile, tile)
        part = jnp.dot(
            binned_ref[pl.ds(base, tile), :], tail_ref[...], preferred_element_type=jnp.float32
        )
        rows[pl.ds(base, tile), :] = (total_ref[pl.ds(base, tile), :] + part).astype(jnp.bfloat16)
        pltpu.make_async_copy(
            rows.at[pl.ds(base, tile)], out_hbm.at[pl.ds(base, tile)], sem
        ).start()
        return carry

    lax.fori_loop(0, 8, body, 0)
    wait_for(rows, sem)


def pass_kernel(in_ref, out_ref):
    out_ref[...] = in_ref[...]


def per_device(traces, owner, counts, inline_off, xline_off, phase_cls):
    n_inl, n_xl = lax.axis_size("inl"), lax.axis_size("xl")
    plane = plane_of(n_inl)
    layers = n_inl // plane
    local_blocks, _, samples = traces.shape
    width = XLINES // n_xl
    large = widest(samples)
    last = span_of(PARTS - 1, samples)[1] - span_of(PARTS - 1, samples)[0]
    half = n_inl * BLOCK_TR
    side = IL_DEV * TAPS
    rows = IL_DEV * width
    in_vmem = pl.BlockSpec(memory_space=pltpu.VMEM)
    in_smem = pl.BlockSpec(memory_space=pltpu.SMEM)
    anywhere = pl.BlockSpec(memory_space=pl.ANY)
    table, nav, taps = pl.pallas_call(
        functools.partial(plan_kernel, n_inl),
        out_shape=(
            jax.ShapeDtypeStruct((n_inl + 8, LANES), jnp.int32),
            jax.ShapeDtypeStruct((local_blocks + 1, BLOCK_TR, LANES), jnp.float32),
            jax.ShapeDtypeStruct((TAPS, LANES), jnp.float32),
        ),
        in_specs=[in_vmem] * 5,
        out_specs=(in_vmem, in_vmem, in_vmem),
        compiler_params=pltpu.CompilerParams(vmem_limit_bytes=8 << 20),
    )(
        owner.reshape(1, local_blocks),
        counts.reshape(1, local_blocks),
        inline_off.T,
        xline_off.T,
        phase_cls.T,
    )
    f32, bf16 = jnp.float32, jnp.bfloat16
    scratch = [
        pltpu.VMEM((local_blocks, BLOCK_TR, samples), f32),
        pltpu.VMEM((n_inl, BLOCK_TR, samples), f32),
        pltpu.VMEM((n_inl, BLOCK_TR, samples), f32),
        pltpu.VMEM((layers, CAP * BLOCK_TR, samples), f32),
        pltpu.VMEM((layers, CAP * BLOCK_TR, samples), f32),
        pltpu.VMEM((plane, layers * BLOCK_TR, samples), f32),
        pltpu.VMEM((plane, layers * BLOCK_TR, samples), f32),
        pltpu.VMEM((n_inl, BLOCK_TR, LANES), f32),
        pltpu.VMEM((n_inl, BLOCK_TR, LANES), f32),
        pltpu.VMEM((layers, CAP, BLOCK_TR, LANES), f32),
        pltpu.VMEM((layers, CAP, BLOCK_TR, LANES), f32),
        pltpu.VMEM((plane, layers, BLOCK_TR, LANES), f32),
        pltpu.VMEM((plane, layers, BLOCK_TR, LANES), f32),
        pltpu.VMEM((2 * half, large), bf16),
        pltpu.VMEM((rows, 2 * half), bf16),
        pltpu.VMEM((2, side, 2 * half), f32),
        pltpu.VMEM((2 * side, 2 * half), bf16),
        pltpu.VMEM((samples, 2 * samples), bf16),
        pltpu.VMEM((rows, samples), f32),
        pltpu.VMEM((2, side, samples), f32),
        pltpu.VMEM((2, side, samples), f32),
        pltpu.VMEM((rows, LANES), f32),
        pltpu.VMEM((2, side, LANES), f32),
        pltpu.VMEM((2, side, LANES), f32),
        pltpu.VMEM((BLOCK_TR, LANES), f32),
        pltpu.VMEM((n_xl, BLOCK_TR, LANES), f32),
        pltpu.SemaphoreType.DMA,
        pltpu.SemaphoreType.DMA((2, PARTS)),
        pltpu.SemaphoreType.DMA((2, PARTS)),
        pltpu.SemaphoreType.DMA((2, PARTS)),
        pltpu.SemaphoreType.DMA((2, 3)),
        pltpu.SemaphoreType.DMA((2, PARTS, 2)),
        pltpu.SemaphoreType.DMA((2, 2)),
        pltpu.SemaphoreType.DMA((2, n_xl)),
    ]
    total, tail, binned, flag = pl.pallas_call(
        functools.partial(fast_kernel, n_inl, n_xl),
        out_shape=(
            jax.ShapeDtypeStruct((rows, 2 * samples), f32),
            jax.ShapeDtypeStruct((last, 2 * samples), bf16),
            jax.ShapeDtypeStruct((rows, last), bf16),
            jax.ShapeDtypeStruct((BLOCK_TR, LANES), f32),
        ),
        in_specs=[in_smem, anywhere, in_vmem, in_vmem],
        out_specs=(in_vmem, in_vmem, in_vmem, in_vmem),
        scratch_shapes=scratch,
        compiler_params=pltpu.CompilerParams(
            collective_id=0, has_side_effects=True, vmem_limit_bytes=36 << 20
        ),
    )(table, traces, nav, taps)

    def finish_fast():
        out = pl.pallas_call(
            finish_kernel,
            out_shape=jax.ShapeDtypeStruct((rows, 2 * samples), bf16),
            in_specs=[in_vmem] * 3,
            out_specs=pl.BlockSpec(memory_space=pltpu.HBM),
            scratch_shapes=[pltpu.VMEM((rows, 2 * samples), bf16), pltpu.SemaphoreType.DMA],
            compiler_params=pltpu.CompilerParams(vmem_limit_bytes=53 << 20),
        )(total, binned, tail)
        return out.reshape(IL_DEV, width, 2 * samples)

    def run_padded():
        out = padded_plan(traces, owner, counts, inline_off, xline_off, phase_cls)
        spec = pl.BlockSpec((2, width, 2 * samples), lambda m: (m, 0, 0))
        return pl.pallas_call(
            pass_kernel,
            grid=(IL_DEV // 2,),
            out_shape=jax.ShapeDtypeStruct(out.shape, out.dtype),
            in_specs=[spec],
            out_specs=spec,
            compiler_params=pltpu.CompilerParams(vmem_limit_bytes=12 << 20),
        )(out)

    return lax.cond(flag[0, 0] > 0.5, run_padded, finish_fast)


def solution(mesh):
    return jax.shard_map(
        per_device,
        mesh=mesh,
        in_specs=(
            P(("inl", "xl"), None, None),
            P(("inl", "xl"), None),
            P(("inl", "xl")),
            P(("inl", "xl"), None),
            P(("inl", "xl"), None),
            P(("inl", "xl"), None),
        ),
        out_specs=P("inl", "xl", None),
        check_vma=False,
    )
```

profile of v0, /device:TPU:1, one launch (start us, length us, event | category | flops | bytes accessed | tf_op | source)
XLA Modules:
  0.0 97.2 jit_solution(2333871543284038215)
XLA Ops:
  0.0 1.2 %shard_map.66 = (s32[72,128]{1,0:T(8,128)S(1)}, f32[65,8,128]{2,1,0:T(8,128)S(1)}, f32[8,128]{1,0:T(8,128)S(1)}) custom-call(s32[1,64]{1,0:T(1,128)} %bitcast.27, s32[1,64]{1,0:T(1,128)} %bitcast.26, s32[8,64]{1,0:T(8,128)} %bitcast.21, s32[8,64]{1,0:T(8,128)} %bitcast.22, s32[8,64]{1,0:T(8,128)} %bitcast.23), custom_call_target="tpu_custom_call" | custom-call | tf_op jit(solution)/shard_map/pallas_call | solution.py:843
  1.2 91.3 %shard_map.67 = (f32[1024,2048]{1,0:T(8,128)S(1)}, bf16[128,2048]{1,0:T(8,128)(2,1)S(1)}, bf16[1024,128]{1,0:T(8,128)(2,1)S(1)}, f32[8,128]{1,0:T(8,128)S(1)}) custom-call(s32[72,128]{1,0:T(8,128)S(1)} %get-tuple-element.42.table_ref, f32[64,8,1024]{2,1,0:T(8,128)} %traces_hbm.1, f32[65,8,128]{2,1,0:T(8,128)S(1)} %get-tuple-element.43.nav_ref, ...), custom_call_target="tpu_custom_call" | custom-call | tf_op jit(solution)/shard_map/pallas_call | solution.py:897
  92.6 0.5 slice.3
  93.7 3.3 %conditional.1 = (bf16[16,64,2048]{2,1,0:T(8,128)(2,1)}) conditional(s32[]{:T(128)} %bitcast.13, (f32[1024,2048]{1,0:T(8,128)S(1)}, bf16[1024,128]{1,0:T(8,128)(2,1)S(1)}, bf16[128,2048]{1,0:T(8,128)(2,1)S(1)}) %tuple.11, (s32[64,1]{0,1:T(1,128)}, s32[64,8]{0,1:T(8,128)}, s32[64,8]{0,1:T(8,128)}, s32[64,8]{0,1:T(8,128)}, s32[64]{0:T(128)}, ...), branch_computations={%region_0.0_spmd, %region_1.4_spmd} | conditional | flops 34864 | bytes 329164 | solution.py:936
  93.7 3.1 %branch_0_fun.1 = bf16[1024,2048]{1,0:T(8,128)(2,1)} custom-call(f32[1024,2048]{1,0:T(8,128)S(1)} %get-tuple-element.26.total_ref, bf16[1024,128]{1,0:T(8,128)(2,1)S(1)} %get-tuple-element.27.binned_ref, bf16[128,2048]{1,0:T(8,128)(2,1)S(1)} %get-tuple-element.28.tail_ref), custom_call_target="tpu_custom_call" | custom-call | tf_op jit(solution)/shard_map/cond/branch_0_fun/pallas_call | solution.py:914
where the time goes:
time: 97.3 us; the launch traced here: 97.2 us
  Pallas kernels  95.6 us (98%)
    pallas_call x1, Pallas kernels, per_device(): pl.pallas_call(functools.partial(fast_kernel, n_inl, n_xl), out_shape=(ja...  91.3 us
    pallas_call x1, Pallas kernels, finish_fast(): pl.pallas_call(finish_kernel, out_shape=jax.ShapeDtypeStruct((rows, 2 * s...  3.1 us

commit v1 on v0

--- a/solution.py
+++ b/solution.py
@@ -360,6 +360,8 @@
     return out.reshape(IL_DEV, width, 2 * samples)
 
 
+OWN_LANE = 4 * BLOCK_TR
+OVER_LANE = OWN_LANE + 1
 EDGES = (0, 3, 5, 7, 8)
 PARTS = len(EDGES) - 1
 
@@ -413,13 +415,19 @@
     trace_idx = lax.broadcasted_iota(jnp.int32, (BLOCK_TR, blocks), 0)
     fields = [inl_ref[...], xl_ref[...], cls_ref[...], (trace_idx < counts_ref[...]).astype(jnp.int32)]
     fields = [field.astype(jnp.float32) for field in fields]
-    field_id = lax.broadcasted_iota(jnp.int32, (BLOCK_TR, LANES), 1)
+    unused = jnp.zeros((LANES - len(fields) * BLOCK_TR, blocks), jnp.float32)
+    columns = jnp.concatenate(fields + [unused], axis=0)
+    same_row = lax.broadcasted_iota(jnp.int32, (blocks, blocks), 0)
+    same_col = lax.broadcasted_iota(jnp.int32, (blocks, blocks), 1)
+    flat = lax.dot_general(
+        jnp.where(same_row == same_col, 1.0, 0.0),
+        columns,
+        (((1,), (1,)), ((), ())),
+        preferred_element_type=jnp.float32,
+    )
     for block in range(blocks):
-        tile = jnp.zeros((BLOCK_TR, LANES), jnp.float32)
-        for place, field in enumerate(fields):
-            tile = jnp.where(field_id == place, field[:, block : block + 1], tile)
-        nav_ref[block] = tile
-    nav_ref[blocks] = jnp.zeros((BLOCK_TR, LANES), jnp.float32)
+        nav_ref[block] = flat[block : block + 1]
+    nav_ref[blocks] = jnp.zeros((1, LANES), jnp.float32)
 
 
 def fast_kernel(
@@ -446,6 +454,8 @@
     z_nav_recv,
     y_nav_send,
     y_nav_recv,
+    z_own,
+    nav_rows,
     samples_in,
     inner,
     outer_f32,
@@ -497,7 +507,7 @@
         other = lax.rem(band + step, n_xl)
         pl.semaphore_signal(barrier, inc=1, device_id={"xl": other}, device_id_type=MESH)
 
-    field_id = lax.broadcasted_iota(jnp.int32, (BLOCK_TR, LANES), 1)
+    field_id = lax.broadcasted_iota(jnp.int32, (1, LANES), 1)
     over = table_ref[n_inl + 2, 0].astype(jnp.float32)
     load.wait()
 
@@ -506,7 +516,7 @@
             spot = layer_to * CAP + r
             block = table_ref[n_inl, spot]
             target = table_ref[n_inl + 1, spot].astype(jnp.float32)
-            z_nav_send[layer_to, r] = jnp.where(field_id == 4, target, nav_ref[block])
+            z_nav_send[layer_to, r] = jnp.where(field_id == OWN_LANE, target, nav_ref[block])
             z_send[layer_to, r * BLOCK_TR : (r + 1) * BLOCK_TR, :] = traces[
                 jnp.minimum(block, blocks - 1)
             ]
@@ -517,7 +527,7 @@
     def gather_first(off, carry):
         dest = lax.rem(me + off, n_inl)
         block = table_ref[dest, 0]
-        p_nav_send[dest] = jnp.where(field_id == 5, over, nav_ref[block])
+        p_nav_send[dest] = jnp.where(field_id == OVER_LANE, over, nav_ref[block])
         p_send[dest] = traces[jnp.minimum(block, blocks - 1)]
         return carry
 
@@ -532,6 +542,13 @@
     def span(c):
         lo, hi = span_of(c, length)
         return pl.ds(lo, hi - lo)
+
+    def away(off):
+        reach = (off + 1) // 2
+        return lax.rem(layer + jnp.where(lax.rem(off, 2) == 1, reach, layers - reach), layers)
+
+    def partner(off):
+        return away(lax.rem(off, layers)) * plane + lax.rem(place + off // layers, plane)
 
     def push(source, target, sems, to):
         pltpu.make_async_remote_copy(
@@ -545,7 +562,7 @@
 
     def push_first(c):
         def body(off, carry):
-            dest = lax.rem(me + off, n_inl)
+            dest = partner(off)
             push(
                 p_send.at[dest, :, span(c)],
                 p_recv.at[me, :, span(c)],
@@ -558,7 +575,7 @@
 
     def push_second(c):
         def body(off, carry):
-            to = lax.rem(layer + off, layers)
+            to = away(off)
             push(
                 z_send.at[to, :, span(c)],
                 z_recv.at[layer, :, span(c)],
@@ -578,7 +595,7 @@
             for origin in range(layers):
                 held = jnp.zeros((BLOCK_TR, hi - lo), jnp.float32)
                 for r in range(CAP):
-                    named = z_nav_recv[origin, r, :, 4:5] == wanted
+                    named = z_own[origin, r, :, 0:1] == wanted
                     value = z_recv[origin, r * BLOCK_TR : (r + 1) * BLOCK_TR, lo:hi]
                     held = jnp.where(named, value, held)
                 y_send[to, origin * BLOCK_TR : (origin + 1) * BLOCK_TR, lo:hi] = held
@@ -629,13 +646,17 @@
 
     wait_for(z_nav_recv.at[pl.ds(0, layers - 1)], nav_sems.at[1, 1])
 
+    for origin in range(layers):
+        for r in range(CAP):
+            own = z_nav_recv[origin, r][:, OWN_LANE : OWN_LANE + 1]
+            z_own[origin, r] = jnp.broadcast_to(own, (BLOCK_TR, LANES))
+
     def spread_nav(to, carry):
         wanted = (to + 1).astype(jnp.float32)
         for origin in range(layers):
-            held = jnp.zeros((BLOCK_TR, LANES), jnp.float32)
+            held = jnp.zeros((1, LANES), jnp.float32)
             for r in range(CAP):
-                tile = z_nav_recv[origin, r]
-                held = jnp.where(tile[:, 4:5] == wanted, tile, held)
+                held = jnp.where(z_own[origin, r, 0:1, 0:1] == wanted, z_nav_recv[origin, r], held)
             y_nav_send[to, origin] = held
         return carry
 
@@ -662,12 +683,31 @@
 
     wait_for(p_nav_recv.at[pl.ds(0, n_inl - 1)], nav_sems.at[1, 0])
     wait_for(y_nav_recv.at[pl.ds(0, plane - 1)], nav_sems.at[1, 2])
-    first_nav = p_nav_recv[...].reshape(half, LANES).T
-    second_nav = y_nav_recv[...].reshape(half, LANES).T
-    nav = jnp.concatenate([first_nav[:8], second_nav[:8]], axis=1)
-    inl_ids, xl_ids, cls_ids, live = nav[0:1], nav[1:2], nav[2:3], nav[3:4]
-
-    seen = jnp.max(first_nav[5:6], axis=1, keepdims=True)
+    def first_row(row, carry):
+        nav_rows[pl.ds(row, 1), :] = p_nav_recv[row]
+        return carry
+
+    lax.fori_loop(0, n_inl, first_row, 0)
+
+    def second_row(origin, carry):
+        for to in range(plane):
+            nav_rows[pl.ds(n_inl + to * layers + origin, 1), :] = y_nav_recv[to, origin]
+        return carry
+
+    lax.fori_loop(0, layers, second_row, 0)
+    column = lax.broadcasted_iota(jnp.int32, (LANES, depth), 1)
+    source = lax.broadcasted_iota(jnp.int32, (LANES, depth), 0)
+    owner_row = lax.broadcasted_iota(jnp.int32, (2 * n_inl, depth), 0)
+    owner_col = lax.broadcasted_iota(jnp.int32, (2 * n_inl, depth), 1)
+    lines = []
+    for field in range(4):
+        pick = jnp.where(source == field * BLOCK_TR + column % BLOCK_TR, 1.0, 0.0)
+        wide = jnp.dot(nav_rows[...], pick, preferred_element_type=jnp.float32)
+        mine = jnp.where(owner_row == owner_col // BLOCK_TR, wide, 0.0)
+        lines.append(jnp.sum(mine, axis=0, keepdims=True))
+    inl_ids, xl_ids, cls_ids, live = lines
+
+    seen = jnp.max(nav_rows[:n_inl, :], axis=0, keepdims=True)[:, OVER_LANE : OVER_LANE + 1]
     flag_send[...] = jnp.broadcast_to(seen, (BLOCK_TR, LANES))
     flag_recv[0] = flag_send[...]
     for step in range(1, n_xl):
@@ -844,7 +884,7 @@
         functools.partial(plan_kernel, n_inl),
         out_shape=(
             jax.ShapeDtypeStruct((n_inl + 8, LANES), jnp.int32),
-            jax.ShapeDtypeStruct((local_blocks + 1, BLOCK_TR, LANES), jnp.float32),
+            jax.ShapeDtypeStruct((local_blocks + 1, 1, LANES), jnp.float32),
             jax.ShapeDtypeStruct((TAPS, LANES), jnp.float32),
         ),
         in_specs=[in_vmem] * 5,
@@ -866,12 +906,14 @@
         pltpu.VMEM((layers, CAP * BLOCK_TR, samples), f32),
         pltpu.VMEM((plane, layers * BLOCK_TR, samples), f32),
         pltpu.VMEM((plane, layers * BLOCK_TR, samples), f32),
-        pltpu.VMEM((n_inl, BLOCK_TR, LANES), f32),
-        pltpu.VMEM((n_inl, BLOCK_TR, LANES), f32),
+        pltpu.VMEM((n_inl, 1, LANES), f32),
+        pltpu.VMEM((n_inl, 1, LANES), f32),
+        pltpu.VMEM((layers, CAP, 1, LANES), f32),
+        pltpu.VMEM((layers, CAP, 1, LANES), f32),
+        pltpu.VMEM((plane, layers, 1, LANES), f32),
+        pltpu.VMEM((plane, layers, 1, LANES), f32),
         pltpu.VMEM((layers, CAP, BLOCK_TR, LANES), f32),
-        pltpu.VMEM((layers, CAP, BLOCK_TR, LANES), f32),
-        pltpu.VMEM((plane, layers, BLOCK_TR, LANES), f32),
-        pltpu.VMEM((plane, layers, BLOCK_TR, LANES), f32),
+        pltpu.VMEM((2 * n_inl, LANES), f32),
         pltpu.VMEM((2 * half, large), bf16),
         pltpu.VMEM((rows, 2 * half), bf16),
         pltpu.VMEM((2, side, 2 * half), f32),

time: 97.3 us -> 90.5 us (0.930)
  Pallas kernels: 95.6 us -> 88.8 us
    pallas_call x1, Pallas kernels: 91.3 us -> 84.7 us  [per_device(): pl.pallas_call(functools.partial(fast_kernel, n_inl, n_xl), out_shape=(ja...]
where the time goes in v1:
time: 90.5 us; the launch traced here: 90.3 us
  Pallas kernels  88.8 us (98%)
    pallas_call x1, Pallas kernels, per_device(): pl.pallas_call(functools.partial(fast_kernel, n_inl, n_xl), out_shape=(ja...  84.7 us
    pallas_call x1, Pallas kernels, finish_fast(): pl.pallas_call(finish_kernel, out_shape=jax.ShapeDtypeStruct((rows, 2 * s...  3.09 us

profile of v1, /device:TPU:1, one launch (start us, length us, event | category | flops | bytes accessed | tf_op | source)
XLA Modules:
  0.0 90.3 jit_solution(4577648044272964491)
XLA Ops:
  0.0 1.0 %shard_map.66 = (s32[72,128]{1,0:T(8,128)S(1)}, f32[65,1,128]{2,1,0:T(1,128)S(1)}, f32[8,128]{1,0:T(8,128)S(1)}) custom-call(s32[1,64]{1,0:T(1,128)} %bitcast.27, s32[1,64]{1,0:T(1,128)} %bitcast.26, s32[8,64]{1,0:T(8,128)} %bitcast.21, s32[8,64]{1,0:T(8,128)} %bitcast.22, s32[8,64]{1,0:T(8,128)} %bitcast.23), custom_call_target="tpu_custom_call" | custom-call | tf_op jit(solution)/shard_map/pallas_call | solution.py:883
  1.0 84.7 %shard_map.67 = (f32[1024,2048]{1,0:T(8,128)S(1)}, bf16[128,2048]{1,0:T(8,128)(2,1)S(1)}, bf16[1024,128]{1,0:T(8,128)(2,1)S(1)}, f32[8,128]{1,0:T(8,128)S(1)}) custom-call(s32[72,128]{1,0:T(8,128)S(1)} %get-tuple-element.42.table_ref, f32[64,8,1024]{2,1,0:T(8,128)} %traces_hbm.1, f32[65,1,128]{2,1,0:T(1,128)S(1)} %get-tuple-element.43.nav_ref, ...), custom_call_target="tpu_custom_call" | custom-call | tf_op jit(solution)/shard_map/pallas_call | solution.py:939
  85.7 0.5 slice.3
  86.9 3.3 %conditional.1 = (bf16[16,64,2048]{2,1,0:T(8,128)(2,1)}) conditional(s32[]{:T(128)} %bitcast.13, (f32[1024,2048]{1,0:T(8,128)S(1)}, bf16[1024,128]{1,0:T(8,128)(2,1)S(1)}, bf16[128,2048]{1,0:T(8,128)(2,1)S(1)}) %tuple.11, (s32[64,1]{0,1:T(1,128)}, s32[64,8]{0,1:T(8,128)}, s32[64,8]{0,1:T(8,128)}, s32[64,8]{0,1:T(8,128)}, s32[64]{0:T(128)}, ...), branch_computations={%region_0.0_spmd, %region_1.4_spmd} | conditional | flops 34864 | bytes 329164 | solution.py:978
  86.9 3.1 %branch_0_fun.1 = bf16[1024,2048]{1,0:T(8,128)(2,1)} custom-call(f32[1024,2048]{1,0:T(8,128)S(1)} %get-tuple-element.26.total_ref, bf16[1024,128]{1,0:T(8,128)(2,1)S(1)} %get-tuple-element.27.binned_ref, bf16[128,2048]{1,0:T(8,128)(2,1)S(1)} %get-tuple-element.28.tail_ref), custom_call_target="tpu_custom_call" | custom-call | tf_op jit(solution)/shard_map/cond/branch_0_fun/pallas_call | solution.py:956

commit v2 on v1

--- a/solution.py
+++ b/solution.py
@@ -378,7 +378,7 @@
     return 8 if n_inl % 8 == 0 and n_inl > 8 else 2
 
 
-def plan_kernel(n_inl, owner_ref, counts_ref, inl_ref, xl_ref, cls_ref, table_ref, nav_ref, taps_ref):
+def make_plan(n_inl, owner_ref, counts_ref, inl_ref, xl_ref, cls_ref, table_ref, nav_ref, taps_ref):
     blocks = owner_ref.shape[1]
     plane = plane_of(n_inl)
     named = owner_ref[...] == lax.broadcasted_iota(jnp.int32, (n_inl, blocks), 0)
@@ -433,14 +433,20 @@
 def fast_kernel(
     n_inl,
     n_xl,
-    table_ref,
+    owner_ref,
+    counts_ref,
+    inl_ref,
+    xl_ref,
+    cls_ref,
     traces_hbm,
-    nav_ref,
-    taps_ref,
     total,
     tail_ref,
     binned_ref,
     flag_ref,
+    table_vmem,
+    table_ref,
+    nav_ref,
+    taps_ref,
     traces,
     p_send,
     p_recv,
@@ -470,6 +476,7 @@
     flag_send,
     flag_recv,
     load_sem,
+    table_sem,
     p_sems,
     z_sems,
     y_sems,
@@ -508,13 +515,17 @@
         pl.semaphore_signal(barrier, inc=1, device_id={"xl": other}, device_id_type=MESH)
 
     field_id = lax.broadcasted_iota(jnp.int32, (1, LANES), 1)
+    make_plan(n_inl, owner_ref, counts_ref, inl_ref, xl_ref, cls_ref, table_vmem, nav_ref, taps_ref)
+    table = pltpu.make_async_copy(table_vmem, table_ref, table_sem)
+    table.start()
+    load.wait()
+    table.wait()
     over = table_ref[n_inl + 2, 0].astype(jnp.float32)
-    load.wait()
 
     def gather_second(layer_to, carry):
         for r in range(CAP):
             spot = layer_to * CAP + r
-            block = table_ref[n_inl, spot]
+            block = jnp.clip(table_ref[n_inl, spot], 0, blocks)
             target = table_ref[n_inl + 1, spot].astype(jnp.float32)
             z_nav_send[layer_to, r] = jnp.where(field_id == OWN_LANE, target, nav_ref[block])
             z_send[layer_to, r * BLOCK_TR : (r + 1) * BLOCK_TR, :] = traces[
@@ -526,7 +537,7 @@
 
     def gather_first(off, carry):
         dest = lax.rem(me + off, n_inl)
-        block = table_ref[dest, 0]
+        block = jnp.clip(table_ref[dest, 0], 0, blocks)
         p_nav_send[dest] = jnp.where(field_id == OVER_LANE, over, nav_ref[block])
         p_send[dest] = traces[jnp.minimum(block, blocks - 1)]
         return carry
@@ -878,27 +889,13 @@
     side = IL_DEV * TAPS
     rows = IL_DEV * width
     in_vmem = pl.BlockSpec(memory_space=pltpu.VMEM)
-    in_smem = pl.BlockSpec(memory_space=pltpu.SMEM)
     anywhere = pl.BlockSpec(memory_space=pl.ANY)
-    table, nav, taps = pl.pallas_call(
-        functools.partial(plan_kernel, n_inl),
-        out_shape=(
-            jax.ShapeDtypeStruct((n_inl + 8, LANES), jnp.int32),
-            jax.ShapeDtypeStruct((local_blocks + 1, 1, LANES), jnp.float32),
-            jax.ShapeDtypeStruct((TAPS, LANES), jnp.float32),
-        ),
-        in_specs=[in_vmem] * 5,
-        out_specs=(in_vmem, in_vmem, in_vmem),
-        compiler_params=pltpu.CompilerParams(vmem_limit_bytes=8 << 20),
-    )(
-        owner.reshape(1, local_blocks),
-        counts.reshape(1, local_blocks),
-        inline_off.T,
-        xline_off.T,
-        phase_cls.T,
-    )
     f32, bf16 = jnp.float32, jnp.bfloat16
     scratch = [
+        pltpu.VMEM((n_inl + 8, LANES), jnp.int32),
+        pltpu.SMEM((n_inl + 8, LANES), jnp.int32),
+        pltpu.VMEM((local_blocks + 1, 1, LANES), f32),
+        pltpu.VMEM((TAPS, LANES), f32),
         pltpu.VMEM((local_blocks, BLOCK_TR, samples), f32),
         pltpu.VMEM((n_inl, BLOCK_TR, samples), f32),
         pltpu.VMEM((n_inl, BLOCK_TR, samples), f32),
@@ -928,6 +925,7 @@
         pltpu.VMEM((BLOCK_TR, LANES), f32),
         pltpu.VMEM((n_xl, BLOCK_TR, LANES), f32),
         pltpu.SemaphoreType.DMA,
+        pltpu.SemaphoreType.DMA,
         pltpu.SemaphoreType.DMA((2, PARTS)),
         pltpu.SemaphoreType.DMA((2, PARTS)),
         pltpu.SemaphoreType.DMA((2, PARTS)),
@@ -944,13 +942,20 @@
             jax.ShapeDtypeStruct((rows, last), bf16),
             jax.ShapeDtypeStruct((BLOCK_TR, LANES), f32),
         ),
-        in_specs=[in_smem, anywhere, in_vmem, in_vmem],
+        in_specs=[in_vmem] * 5 + [anywhere],
         out_specs=(in_vmem, in_vmem, in_vmem, in_vmem),
         scratch_shapes=scratch,
         compiler_params=pltpu.CompilerParams(
             collective_id=0, has_side_effects=True, vmem_limit_bytes=36 << 20
         ),
-    )(table, traces, nav, taps)
+    )(
+        owner.reshape(1, local_blocks),
+        counts.reshape(1, local_blocks),
+        inline_off.T,
+        xline_off.T,
+        phase_cls.T,
+        traces,
+    )
 
     def finish_fast():
         out = pl.pallas_call(

time: 90.5 us -> 88.6 us (0.979)
  Pallas kernels: 88.8 us -> 87 us
    pallas_call x1 -> x0, Pallas kernels: 0.99 us -> none  [per_device(): pl.pallas_call(functools.partial(plan_kernel, n_inl), out_shape=(jax.Shap...]
where the time goes in v2:
time: 88.6 us; the launch traced here: 88.5 us
  Pallas kernels  87 us (98%)
    pallas_call x1, Pallas kernels, per_device(): pl.pallas_call(functools.partial(fast_kernel, n_inl, n_xl), out_shape=(ja...  83.9 us
    pallas_call x1, Pallas kernels, finish_fast(): pl.pallas_call(finish_kernel, out_shape=jax.ShapeDtypeStruct((rows, 2 * s...  3.1 us

profile of v2, /device:TPU:1, one launch (start us, length us, event | category | flops | bytes accessed | tf_op | source)
XLA Modules:
  0.0 88.5 jit_solution(11965606248585013847)
XLA Ops:
  0.0 83.9 %shard_map.66 = (f32[1024,2048]{1,0:T(8,128)S(1)}, bf16[128,2048]{1,0:T(8,128)(2,1)S(1)}, bf16[1024,128]{1,0:T(8,128)(2,1)S(1)}, f32[8,128]{1,0:T(8,128)S(1)}) custom-call(s32[1,64]{1,0:T(1,128)} %bitcast.27, s32[1,64]{1,0:T(1,128)} %bitcast.26, s32[8,64]{1,0:T(8,128)} %bitcast.21, s32[8,64]{1,0:T(8,128)} %bitcast.22, s32[8,64]{1,0:T(8,128)} %bitcast.23, ...), custom_call_target="tpu_custom_call" | custom-call | tf_op jit(solution)/shard_map/pallas_call | solution.py:937
  83.9 0.5 slice.3
  85.0 3.3 %conditional.1 = (bf16[16,64,2048]{2,1,0:T(8,128)(2,1)}) conditional(s32[]{:T(128)} %bitcast.13, (f32[1024,2048]{1,0:T(8,128)S(1)}, bf16[1024,128]{1,0:T(8,128)(2,1)S(1)}, bf16[128,2048]{1,0:T(8,128)(2,1)S(1)}) %tuple.11, (s32[64,1]{0,1:T(1,128)}, s32[64,8]{0,1:T(8,128)}, s32[64,8]{0,1:T(8,128)}, s32[64,8]{0,1:T(8,128)}, s32[64]{0:T(128)}, ...), branch_computations={%region_0.0_spmd, %region_1.4_spmd} | conditional | flops 34864 | bytes 329164 | solution.py:983
  85.1 3.1 %branch_0_fun.1 = bf16[1024,2048]{1,0:T(8,128)(2,1)} custom-call(f32[1024,2048]{1,0:T(8,128)S(1)} %get-tuple-element.26.total_ref, bf16[1024,128]{1,0:T(8,128)(2,1)S(1)} %get-tuple-element.27.binned_ref, bf16[128,2048]{1,0:T(8,128)(2,1)S(1)} %get-tuple-element.28.tail_ref), custom_call_target="tpu_custom_call" | custom-call | tf_op jit(solution)/shard_map/cond/branch_0_fun/pallas_call | solution.py:961
